TPU v7x, 32 devices: a whole 2x2x4 slice. The times are simulated.
32 devices in a mesh: lon: 4 (over y, x), lat: 8 (over z, core).
Axes of the slice: x: 2, y: 2, z: 4, core: 2. Of those that a mesh axis runs over, the one named last changes fastest.
Arguments:
- tracer: float32 [1024, 64, 128], P('lon', 'lat'), may hold values from -6 to 6
- offsets: int32 [64], P('lat'), may hold values from 0 to 1023
- frac_lon: float32 [64], P('lat'), may hold values from 0 to 1
- frac_lat: float32 [64], P('lat'), may hold values from 0 to 1
- frac_lev: float32 [64], P('lat'), may hold values from 0 to 1
- metric: float32 [64], P('lat'), may hold values from 0.5 to 2
- vertical_coef: float32 [128], replicated, may hold values from 0.5 to 4
- inverses: float32 [64, 128, 128], P('lat'), may hold values from -0.1 to 0.6, as said below
Outputs:
- advected: float32 [1024, 64, 128], P('lon', 'lat')
- pressure: float32 [1024, 64, 128], P('lon', 'lat')
- residual: float32 [1024, 64, 128], P('lon', 'lat')
Inputs may be any that keep to these rules, and one draw needn't show every extreme that they name: `inverses`: one matrix for each latitude row.
All inputs are finite; a program needn't handle non-finite values.
Results may differ from a plain program's by a relative error of at most 0.00016.
Values sent between devices are 32-bit elements; how exact they have to be, the bound alone decides.
A program may use at most 128 MiB of HBM per device.

v0:
```python
import functools

import jax
import jax.numpy as jnp
from jax import lax
from jax.experimental import pallas as pl
from jax.experimental.pallas import tpu as pltpu
from jax.sharding import PartitionSpec as P

ITERS = 3
VM = pl.BlockSpec(memory_space=pltpu.VMEM)
SM = pl.BlockSpec(memory_space=pltpu.SMEM)
F32 = jnp.float32


def cubic_weights(f):
    return (
        -f * (f - 1.0) * (f - 2.0) * (1.0 / 6.0),
        (f + 1.0) * (f - 1.0) * (f - 2.0) * 0.5,
        -(f + 1.0) * f * (f - 2.0) * 0.5,
        (f + 1.0) * f * (f - 1.0) * (1.0 / 6.0),
    )


def shape(*dims):
    return jax.ShapeDtypeStruct(dims, F32)


def mix_kernel(rows, fr_lat, fr_lev, t_ref, prev_ref, next_ref, out_ref):
    width, levels = prev_ref.shape
    lane = lax.broadcasted_iota(jnp.int32, (1, levels), 1)
    row = [prev_ref[...]]
    row += [t_ref[pl.ds(j, width, stride=rows), :] for j in range(2)]
    for j in range(rows):
        if j + 2 < rows:
            row.append(t_ref[pl.ds(j + 2, width, stride=rows), :])
        else:
            row.append(next_ref[j + 2 - rows])
        a = cubic_weights(fr_lat[j])
        b = cubic_weights(fr_lev[j])
        lat = a[0] * row[j] + a[1] * row[j + 1] + a[2] * row[j + 2] + a[3] * row[j + 3]
        total = b[1] * lat
        for m in (-1, 1, 2):
            inside = (lane + m >= 0) & (lane + m < levels)
            weight = jnp.where(inside, b[m + 1], 0.0)
            total = total + weight * pltpu.roll(lat, (-m) % levels, 1)
        out_ref[j] = total


def roll_kernel(rows, cells, out, chunk, off, fr, base, in_ref, out_ref, pad):
    for r in range(rows):
        pad[r, :cells, :] = in_ref[r]
        pad[r, cells:, :] = in_ref[r, : chunk + 8, :]
        w = cubic_weights(fr[r])

        def step(c, carry):
            first = c * chunk
            start = lax.rem(base[0] + first - off[r] - 1 + 2 * cells, cells)
            total = w[0] * pad[r, pl.ds(start, chunk), :]
            for m in range(1, 4):
                total = total + w[m] * pad[r, pl.ds(start + m, chunk), :]
            out_ref[r, pl.ds(pl.multiple_of(first, chunk), chunk), :] = total
            return carry

        lax.fori_loop(0, out // chunk, step, 0)


def split(x):
    high = x.astype(jnp.bfloat16)
    return high, (x - high.astype(F32)).astype(jnp.bfloat16)


def solve_lines(inv, v):
    ih, il = split(inv)
    vh, vl = split(v)
    dot = lambda p, q: lax.dot_general(p, q, (((1,), (1,)), ((), ())), preferred_element_type=F32)
    return dot(vh, ih) + (dot(vh, il) + dot(vl, ih))


def put(refs, j, rows, w):
    w_ref, first, last, low, high = refs
    w_ref[j] = w
    low[j : j + 1, :] = w[:1]
    high[j : j + 1, :] = w[-1:]
    if j == 0:
        first[...] = w
    if j == rows - 1:
        last[...] = w


def line_kernel(rows, inv_ref, r_ref, *outs):
    for j in range(rows):
        put(outs, j, rows, solve_lines(inv_ref[j], r_ref[j]))


def apply_row(j, rows, metric, vc_ref, w_ref, prev, nxt, west, east, pad):
    width, levels = prev.shape
    lane = lax.broadcasted_iota(jnp.int32, (1, levels), 1)
    vc = vc_ref[...]
    up = jnp.where(lane < levels - 1, vc, 0.0)
    down = jnp.where(lane > 0, vc, 0.0)
    w = w_ref[j]
    pad[7:8, :] = west[j : j + 1, :]
    pad[8 : 8 + width, :] = w
    pad[8 + width : 9 + width, :] = east[j : j + 1, :]
    south = prev[...] if j == 0 else w_ref[j - 1]
    north = nxt[...] if j == rows - 1 else w_ref[j + 1]
    m = metric[j]
    result = (2.0 * m + 2.1 + 2.0 * vc) * w
    result = result - m * (pad[9 : 9 + width, :] + pad[7 : 7 + width, :])
    result = result - (south + north)
    result = result - up * pltpu.roll(w, levels - 1, 1)
    return result - down * pltpu.roll(w, 1, 1)


def apply_kernel(rows, metric, vc, inv_ref, w_ref, prev, nxt, west, east, v_ref, *rest):
    outs, pad = rest[:-1], rest[-1]
    for j in range(rows):
        v = apply_row(j, rows, metric, vc, w_ref, prev, nxt, west, east, pad.at[j % 2])
        v_ref[j] = v
        put(outs, j, rows, solve_lines(inv_ref[j], v))


def last_kernel(rows, metric, vc, r_ref, v0_ref, v1_ref, w_ref, prev, nxt, west, east, v_ref, sums, pad):
    levels = prev.shape[1]
    acc = [jnp.zeros((1, levels), F32) for _ in range(9)]
    for j in range(rows):
        v2 = apply_row(j, rows, metric, vc, w_ref, prev, nxt, west, east, pad.at[j % 2])
        v_ref[j] = v2
        r, v0, v1 = r_ref[j], v0_ref[j], v1_ref[j]
        pairs = [(r, v0), (r, v1), (r, v2), (v0, v0), (v0, v1), (v0, v2), (v1, v1), (v1, v2), (v2, v2)]
        for n, (p, q) in enumerate(pairs):
            acc[n] = acc[n] + jnp.sum(p * q, axis=0, keepdims=True)
    for n in range(9):
        sums[n : n + 1, :] = acc[n]
    sums[9:, :] = jnp.zeros((7, levels), F32)


def coefficients(t):
    right = t[:3]
    gram = [[t[3], t[4], t[5]], [t[4], t[6], t[7]], [t[5], t[7], t[8]]]
    zero = jnp.zeros_like(t[0])

    def form(p, q):
        total = zero
        for k in range(3):
            for l in range(3):
                if p[k] is not None and q[l] is not None:
                    total = total + p[k] * q[l] * gram[k][l]
        return total

    def add(p, s, q):
        return [x if y is None else (s * y if x is None else x + s * y) for x, y in zip(p, q)]

    q = [[zero + 1.0, None, None]]
    rho, pi = [None] * 3, [None] * 3
    squares = [form(q[0], q[0])]
    for i in range(ITERS):
        along = form(q[i], rho)
        for k in range(3):
            if q[i][k] is not None:
                along = along + q[i][k] * right[k]
        alpha = along / squares[i]
        pi = add(pi, alpha, q[i])
        rho = add(rho, -alpha, q[i])
        if i + 1 < ITERS:
            z = [zero + 1.0, rho[0], rho[1]]
            new = z
            for l in range(i + 1):
                new = add(new, -form(z, q[l]) / squares[l], q[l])
            q.append(new)
            squares.append(form(new, new))
    return rho, pi


def final_kernel(rows, all_ref, r_ref, v0, v1, v2, w0, w1, w2, a_out, p_out, r_out):
    width = r_ref.shape[1]
    total = jnp.sum(jnp.sum(all_ref[...], axis=0), axis=1, keepdims=True)
    rho, pi = coefficients([total[n : n + 1, :] for n in range(9)])
    for j in range(rows):
        r = r_ref[j]
        where = pl.ds(j, width, stride=rows)
        a_out[where, :] = r
        p_out[where, :] = pi[0] * w0[j] + pi[1] * w1[j] + pi[2] * w2[j]
        r_out[where, :] = r + (rho[0] * v0[j] + rho[1] * v1[j] + rho[2] * v2[j])


def call(kernel, outs, ins, scratch=()):
    return pl.pallas_call(
        kernel,
        out_shape=outs,
        in_specs=ins,
        out_specs=jax.tree.map(lambda _: VM, outs),
        scratch_shapes=list(scratch),
    )


def body(tracer, offsets, frac_lon, frac_lat, frac_lev, metric, vertical_coef, inverses):
    width, rows, levels = tracer.shape
    lons, lats = lax.axis_size("lon"), lax.axis_size("lat")
    cells = width * lons
    up = [(i, i + 1) for i in range(lats - 1)]
    down = [(i + 1, i) for i in range(lats - 1)]
    east = [(i, (i + 1) % lons) for i in range(lons)]
    west = [((i + 1) % lons, i) for i in range(lons)]
    flat = tracer.reshape(width * rows, levels)
    prev = lax.ppermute(tracer[:, rows - 1, :], "lat", up)
    nxt = lax.ppermute(jnp.stack([tracer[:, 0, :], tracer[:, 1, :]]), "lat", down)
    cube = shape(rows, width, levels)
    mixed = call(functools.partial(mix_kernel, rows), cube, [SM, SM, VM, VM, VM])(
        frac_lat, frac_lev, flat, prev, nxt
    )
    chunk = min(128, width)
    lon = lax.axis_index("lon")
    if rows % lons == 0:
        some = rows // lons
        piece = lax.all_to_all(mixed, "lon", 0, 1, tiled=True)
        mine = lambda x: lax.dynamic_slice_in_dim(x, lon * some, some)
        args = (mine(offsets), mine(frac_lon), jnp.zeros((1,), jnp.int32))
        out = cells
    else:
        some = rows
        piece = lax.all_gather(mixed, "lon", axis=1, tiled=True)
        args = (offsets, frac_lon, (lon * width).reshape(1).astype(jnp.int32))
        out = width
    turned = call(
        functools.partial(roll_kernel, some, cells, out, chunk),
        shape(some, out, levels),
        [SM, SM, SM, VM],
        [pltpu.VMEM((some, cells + chunk + 8, levels), F32)],
    )(*args, piece)
    if rows % lons == 0:
        turned = lax.all_to_all(turned, "lon", 1, 0, tiled=True)
    r0 = turned
    vc = vertical_coef.reshape(1, levels)
    edge, end = shape(width, levels), shape(rows, levels)
    fields = [cube, edge, edge, end, end]
    pad = [pltpu.VMEM((2, width + 16, levels), F32)]

    def halo(first, last, low, high):
        return (
            lax.ppermute(last, "lat", up),
            lax.ppermute(first, "lat", down),
            lax.ppermute(high, "lon", east),
            lax.ppermute(low, "lon", west),
        )

    w0, *edges = call(functools.partial(line_kernel, rows), fields, [VM, VM])(inverses, r0)
    step = call(functools.partial(apply_kernel, rows), [cube] + fields, [SM] + [VM] * 7, pad)
    v0, w1, *edges = step(metric, vc, inverses, w0, *halo(*edges))
    v1, w2, *edges = step(metric, vc, inverses, w1, *halo(*edges))
    v2, sums = call(
        functools.partial(last_kernel, rows), [cube, shape(16, levels)], [SM] + [VM] * 9, pad
    )(metric, vc, r0, v0, v1, w2, *halo(*edges))
    every = lax.all_gather(sums, ("lon", "lat"))
    whole = shape(width * rows, levels)
    outs = call(functools.partial(final_kernel, rows), [whole] * 3, [VM] * 8)(
        every, r0, v0, v1, v2, w0, w1, w2
    )
    return tuple(x.reshape(width, rows, levels) for x in outs)


def solution(mesh):
    cube = P("lon", "lat", None)
    in_specs = (cube, P("lat"), P("lat"), P("lat"), P("lat"), P("lat"), P(), P("lat", None, None))
    return jax.shard_map(
        body, mesh=mesh, in_specs=in_specs, out_specs=(cube, cube, cube), check_vma=False
    )
```

profile of v0, /device:TPU:0, one launch (start us, length us, event | category | flops | bytes accessed | tf_op | source)
XLA Modules:
  0.0 155.2 jit_solution(18445472859975546920)
XLA Ops:
  0.6 2.4 %fusion = (f32[256,1,128]{2,1,0:T(1,128)S(1)}, f32[256,1,128]{2,1,0:T(1,128)S(1)}, f32[256,1,128]{2,1,0:T(1,128)S(1)}) fusion(f32[256,8,128]{2,1,0:T(8,128)} %param.8), kind=kLoop, calls=%fused_computation.1 | loop fusion | bytes 786432 | tf_op jit(solution)/shard_map/slice | solution.py:208
  3.1 1.3 collective-permute-start.1
  4.4 3.0 %collective-permute-start = (f32[256,128]{1,0:T(8,128)S(1)}, f32[256,128]{1,0:T(8,128)S(1)}, u32[]{:S(2)}, u32[]{:S(2)}) collective-permute-start(f32[256,128]{1,0:T(8,128)S(1)} %bitcast.33), channel_id=1, source_target_pairs={{0,1},{1,2},{2,3},{3,4},{4,5},{5,6},{6,7},{8,9},{9,10},{10,11},{11... | collective-permute-start | bytes 393224 | tf_op jit(solution)/shard_map/ppermute | solution.py:207
  7.4 1.0 collective-permute-done.prev_ref
  8.4 0.0 collective-permute-done.1.next_ref
  8.4 0.6 copy-done.7
  9.0 0.1 copy-done
  9.1 3.3 %shard_map.103 = f32[8,256,128]{2,1,0:T(8,128)} custom-call(f32[8]{0:T(128)} %fr_lat.1, f32[8]{0:T(128)} %fr_lev.1, f32[2048,128]{1,0:T(8,128)} %bitcast.29, f32[256,128]{1,0:T(8,128)} %copy-done.7, f32[2,256,128]{2,1,0:T(8,128)} %copy-done), custom_call_target="tpu_custom_call" | custom-call | tf_op jit(solution)/shard_map/pallas_call | solution.py:210
  12.4 5.2 %all-to-all-start = ((f32[8,256,128]{2,1,0:T(8,128)}), f32[8,256,128]{2,1,0:T(8,128)S(1)}, u32[]{:S(2)}, u32[]{:S(2)}) async-start(f32[8,256,128]{2,1,0:T(8,128)} %shard_map.103), calls=%async_computation | async-start | bytes 2097152 | tf_op jit(solution)/shard_map/all_to_all | solution.py:217
  17.6 0.7 copy-done.17
  18.3 0.6 dynamic_slice.6.off
  18.8 0.1 copy-done.18
  18.9 0.6 dynamic_slice.7.fr
  19.5 12.1 %all-to-all-done = f32[8,256,128]{2,1,0:T(8,128)S(1)} async-done(((f32[8,256,128]{2,1,0:T(8,128)}), f32[8,256,128]{2,1,0:T(8,128)S(1)}, u32[]{:S(2)}, u32[]{:S(2)}) %all-to-all-start) | async-done | bytes 1048608 | tf_op jit(solution)/shard_map/all_to_all | solution.py:217
  31.6 1.0 copy.19
  32.6 2.7 %shard_map.104 = f32[2,1024,128]{2,1,0:T(8,128)} custom-call(s32[2]{0:T(128)} %dynamic_slice.6.off, f32[2]{0:T(128)} %dynamic_slice.7.fr, s32[1]{0:T(128)} %constant.12.clone.1.base, f32[2,1024,128]{2,1,0:T(8,128)} %bitcast.27), custom_call_target="tpu_custom_call" | custom-call | tf_op jit(solution)/shard_map/pallas_call | solution.py:226
  35.4 2.0 %copy.20 = f32[2,1024,128]{2,0,1:T(2,128)S(1)} copy(f32[2,1024,128]{2,1,0:T(8,128)} %shard_map.104) | data formatting | bytes 2097152 | tf_op jit(solution)/shard_map/pallas_call | solution.py:226
  37.4 17.7 %all_to_all.36 = f32[2,1024,128]{2,0,1:T(2,128)S(1)} all-to-all(f32[2,1024,128]{2,0,1:T(2,128)S(1)} %copy.20), channel_id=1, replica_groups=mesh['lon'=4,'lat'=8] {'lon'}, dimensions={1} | all-to-all | bytes 2097152 | tf_op jit(solution)/shard_map/all_to_all | solution.py:233
  55.1 1.0 copy.21
  56.2 3.0 %shard_map.105 = (f32[8,256,128]{2,1,0:T(8,128)}, f32[256,128]{1,0:T(8,128)}, f32[256,128]{1,0:T(8,128)}, f32[8,128]{1,0:T(8,128)}, f32[8,128]{1,0:T(8,128)}) custom-call(f32[8,128,128]{2,1,0:T(8,128)} %inv_ref.5, f32[8,256,128]{2,1,0:T(8,128)} %bitcast.23), custom_call_target="tpu_custom_call" | custom-call | tf_op jit(solution)/shard_map/pallas_call | solution.py:248
  59.1 1.8 %collective-permute-start.2 = (f32[256,128]{1,0:T(8,128)}, f32[256,128]{1,0:T(8,128)S(1)}, u32[]{:S(2)}, u32[]{:S(2)}) collective-permute-start(f32[256,128]{1,0:T(8,128)} %get-tuple-element.26), channel_id=1, source_target_pairs={{0,1},{1,2},{2,3},{3,4},{4,5},{5,6},{6,7},{8,9},{9,10},{10,11},{11... | collective-permute-start | bytes 393224 | tf_op jit(solution)/shard_map/ppermute | solution.py:242
  60.9 1.3 collective-permute-start.3
  62.2 1.3 collective-permute-start.4
  63.5 1.7 %collective-permute-start.5 = (f32[8,128]{1,0:T(8,128)S(1)}, f32[8,128]{1,0:T(8,128)S(1)}, u32[]{:S(2)}, u32[]{:S(2)}) collective-permute-start(f32[8,128]{1,0:T(8,128)S(1)} %copy-done.16), channel_id=1, source_target_pairs={{8,0},{16,8},{24,16},{0,24},{9,1},{17,9},{25,17},{1,25},{10,2},{18... | collective-permute-start | bytes 12296 | tf_op jit(solution)/shard_map/ppermute | solution.py:245
  65.2 1.8 %collective-permute-done.4.west = f32[8,128]{1,0:T(8,128)S(1)} collective-permute-done((f32[8,128]{1,0:T(8,128)}, f32[8,128]{1,0:T(8,128)S(1)}, u32[]{:S(2)}, u32[]{:S(2)}) %collective-permute-start.4) | collective-permute-done | bytes 4128 | tf_op jit(solution)/shard_map/ppermute | solution.py:244
  67.0 0.2 collective-permute-done.5.east
  67.1 0.0 collective-permute-done.2.prev
  67.1 0.0 collective-permute-done.3.nxt
  67.1 0.0 copy-start.3
  67.1 0.4 copy-done.8
  67.6 0.2 copy-done.10
  67.7 0.1 copy-done.1
  67.8 0.0 copy-done.3
  67.8 3.6 %shard_map.106 = (f32[8,256,128]{2,1,0:T(8,128)}, f32[8,256,128]{2,1,0:T(8,128)}, f32[256,128]{1,0:T(8,128)}, f32[256,128]{1,0:T(8,128)}, f32[8,128]{1,0:T(8,128)}, /*index=5*/f32[8,128]{1,0:T(8,128)}) custom-call(f32[8]{0:T(128)} %metric.5, f32[1,128]{1,0:T(1,128)} %bitcast.34, f32[8,128,128]{2,1,0:T(8,128)} %inv_ref.5, ...), custom_call_target="tpu_custom_call" | custom-call | tf_op jit(solution)/shard_map/pallas_call | solution.py:250
  71.4 4.9 %collective-permute-start.6 = (f32[256,128]{1,0:T(8,128)}, f32[256,128]{1,0:T(8,128)S(1)}, u32[]{:S(2)}, u32[]{:S(2)}) collective-permute-start(f32[256,128]{1,0:T(8,128)} %get-tuple-element.32), channel_id=1, source_target_pairs={{0,1},{1,2},{2,3},{3,4},{4,5},{5,6},{6,7},{8,9},{9,10},{10,11},{11... | collective-permute-start | bytes 393224 | tf_op jit(solution)/shard_map/ppermute | solution.py:242
  76.3 1.3 collective-permute-start.7
  77.6 1.0 collective-permute-start.8
  78.7 1.9 %collective-permute-start.9 = (f32[8,128]{1,0:T(8,128)S(1)}, f32[8,128]{1,0:T(8,128)S(1)}, u32[]{:S(2)}, u32[]{:S(2)}) collective-permute-start(f32[8,128]{1,0:T(8,128)S(1)} %copy-done.14), channel_id=1, source_target_pairs={{8,0},{16,8},{24,16},{0,24},{9,1},{17,9},{25,17},{1,25},{10,2},{18... | collective-permute-start | bytes 12296 | tf_op jit(solution)/shard_map/ppermute | solution.py:245
  80.6 1.8 %collective-permute-done.8.west = f32[8,128]{1,0:T(8,128)S(1)} collective-permute-done((f32[8,128]{1,0:T(8,128)}, f32[8,128]{1,0:T(8,128)S(1)}, u32[]{:S(2)}, u32[]{:S(2)}) %collective-permute-start.8) | collective-permute-done | bytes 4128 | tf_op jit(solution)/shard_map/ppermute | solution.py:244
  82.4 0.0 collective-permute-done.9.east
  82.4 0.0 collective-permute-done.6.prev
  82.4 0.0 copy-start.2
  82.4 0.0 collective-permute-done.7.nxt
  82.4 0.0 copy-start.5
  82.5 0.5 copy-done.9
  83.0 0.0 copy-done.12
  83.0 0.1 copy-done.2
  83.1 0.0 copy-done.5
  83.1 3.6 %shard_map.107 = (f32[8,256,128]{2,1,0:T(8,128)}, f32[8,256,128]{2,1,0:T(8,128)}, f32[256,128]{1,0:T(8,128)}, f32[256,128]{1,0:T(8,128)}, f32[8,128]{1,0:T(8,128)}, /*index=5*/f32[8,128]{1,0:T(8,128)}) custom-call(f32[8]{0:T(128)} %metric.5, f32[1,128]{1,0:T(1,128)} %bitcast.35, f32[8,128,128]{2,1,0:T(8,128)} %inv_ref.5, ...), custom_call_target="tpu_custom_call" | custom-call | tf_op jit(solution)/shard_map/pallas_call | solution.py:251
  86.7 4.3 %collective-permute-start.10 = (f32[256,128]{1,0:T(8,128)}, f32[256,128]{1,0:T(8,128)S(1)}, u32[]{:S(2)}, u32[]{:S(2)}) collective-permute-start(f32[256,128]{1,0:T(8,128)} %get-tuple-element.38), channel_id=1, source_target_pairs={{0,1},{1,2},{2,3},{3,4},{4,5},{5,6},{6,7},{8,9},{9,10},{10,11},{11... | collective-permute-start | bytes 393224 | tf_op jit(solution)/shard_map/ppermute | solution.py:242
  91.0 1.3 collective-permute-start.11
  92.3 2.2 %collective-permute-start.12 = (f32[8,128]{1,0:T(8,128)}, f32[8,128]{1,0:T(8,128)S(1)}, u32[]{:S(2)}, u32[]{:S(2)}) collective-permute-start(f32[8,128]{1,0:T(8,128)} %get-tuple-element.40), channel_id=1, source_target_pairs={{0,8},{8,16},{16,24},{24,0},{1,9},{9,17},{17,25},{25,1},{2,10},{10... | collective-permute-start | bytes 12296 | tf_op jit(solution)/shard_map/ppermute | solution.py:244
  94.5 0.8 collective-permute-start.13
  95.3 1.8 %collective-permute-done.12.west = f32[8,128]{1,0:T(8,128)S(1)} collective-permute-done((f32[8,128]{1,0:T(8,128)}, f32[8,128]{1,0:T(8,128)S(1)}, u32[]{:S(2)}, u32[]{:S(2)}) %collective-permute-start.12) | collective-permute-done | bytes 4128 | tf_op jit(solution)/shard_map/ppermute | solution.py:244
  97.1 1.0 collective-permute-done.13.east
  98.1 0.0 collective-permute-done.10.prev
  98.1 0.0 collective-permute-done.11.nxt
  98.1 0.0 copy-start.6
  98.2 0.6 copy-done.13
  98.7 0.1 copy-done.4
  98.8 0.0 copy-done.6
  98.8 4.3 %shard_map.108 = (f32[8,256,128]{2,1,0:T(8,128)}, f32[16,128]{1,0:T(8,128)}) custom-call(f32[8]{0:T(128)} %metric.5, f32[1,128]{1,0:T(1,128)} %bitcast.36, f32[8,256,128]{2,1,0:T(8,128)} %bitcast.24, f32[8,256,128]{2,1,0:T(8,128)} %get-tuple-element.30.v0_ref.v0, f32[8,256,128]{2,1,0:T(8,128)} %get-tuple-element.36.v1_ref.v1, ...), custom_call_target="tpu_custom_call" | custom-call | tf_op jit(solution)/shard_map/pallas_call | solution.py:252
  103.1 46.4 %all-gather = f32[512,128]{1,0:T(8,128)} all-gather(f32[16,128]{1,0:T(8,128)} %get-tuple-element.42), channel_id=2, replica_groups=mesh['lon'=4,'lat'=8] {'lon','lat'}, dimensions={0}, use_global_device_ids=true | all-gather | bytes 270336 | tf_op jit(solution)/shard_map/all_gather | solution.py:255
  149.6 5.7 %shard_map.109 = (f32[2048,128]{1,0:T(8,128)}, f32[2048,128]{1,0:T(8,128)}, f32[2048,128]{1,0:T(8,128)}) custom-call(f32[32,16,128]{2,1,0:T(8,128)} %bitcast.30, f32[8,256,128]{2,1,0:T(8,128)} %bitcast.25, f32[8,256,128]{2,1,0:T(8,128)} %get-tuple-element.30.v0_ref.v0, f32[8,256,128]{2,1,0:T(8,128)} %get-tuple-element.36.v1_ref.v1, ...), custom_call_target="tpu_custom_call" | custom-call | tf_op jit(solution)/shard_map/pallas_call | solution.py:257
  (20 shorter events, 0.1 us)
Async XLA Ops:
  3.1 5.3 %collective-permute-start.1 = (f32[2,256,128]{2,1,0:T(8,128)S(1)}, f32[2,256,128]{2,1,0:T(8,128)S(1)}, u32[]{:S(2)}, u32[]{:S(2)}) collective-permute-start(f32[2,256,128]{2,1,0:T(8,128)S(1)} %pad_maximum_fusion), channel_id=1, source_target_pairs={{1,0},{2,1},{3,2},{4,3},{5,4},{6,5},{7,6},{9,8},{10,9},{11,10},{12... | collective-permute-start | bytes 786440 | tf_op jit(solution)/shard_map/ppermute | solution.py:208
  4.4 4.0 %collective-permute-start = (f32[256,128]{1,0:T(8,128)S(1)}, f32[256,128]{1,0:T(8,128)S(1)}, u32[]{:S(2)}, u32[]{:S(2)}) collective-permute-start(f32[256,128]{1,0:T(8,128)S(1)} %bitcast.33), channel_id=1, source_target_pairs={{0,1},{1,2},{2,3},{3,4},{4,5},{5,6},{6,7},{8,9},{9,10},{10,11},{11... | collective-permute-start | bytes 393224 | tf_op jit(solution)/shard_map/ppermute | solution.py:207
  8.4 0.7 copy-start.7
  8.4 0.7 copy-start
  12.4 19.2 %all-to-all-start = ((f32[8,256,128]{2,1,0:T(8,128)}), f32[8,256,128]{2,1,0:T(8,128)S(1)}, u32[]{:S(2)}, u32[]{:S(2)}) async-start(f32[8,256,128]{2,1,0:T(8,128)} %shard_map.103), calls=%async_computation | async-start | bytes 2097152 | tf_op jit(solution)/shard_map/all_to_all | solution.py:217
  17.6 0.7 copy-start.17
  18.3 0.7 copy-start.18
  59.1 4.4 %copy-start.16 = (f32[8,128]{1,0:T(8,128)S(1)}, f32[8,128]{1,0:T(8,128)}, u32[]{:S(2)}) copy-start(f32[8,128]{1,0:T(8,128)} %get-tuple-element.29) | copy-start | bytes 12292
  59.1 8.0 %collective-permute-start.2 = (f32[256,128]{1,0:T(8,128)}, f32[256,128]{1,0:T(8,128)S(1)}, u32[]{:S(2)}, u32[]{:S(2)}) collective-permute-start(f32[256,128]{1,0:T(8,128)} %get-tuple-element.26), channel_id=1, source_target_pairs={{0,1},{1,2},{2,3},{3,4},{4,5},{5,6},{6,7},{8,9},{9,10},{10,11},{11... | collective-permute-start | bytes 393224 | tf_op jit(solution)/shard_map/ppermute | solution.py:242
  60.9 6.2 %collective-permute-start.3 = (f32[256,128]{1,0:T(8,128)}, f32[256,128]{1,0:T(8,128)S(1)}, u32[]{:S(2)}, u32[]{:S(2)}) collective-permute-start(f32[256,128]{1,0:T(8,128)} %get-tuple-element.27), channel_id=1, source_target_pairs={{1,0},{2,1},{3,2},{4,3},{5,4},{6,5},{7,6},{9,8},{10,9},{11,10},{12... | collective-permute-start | bytes 393224 | tf_op jit(solution)/shard_map/ppermute | solution.py:243
  62.2 4.8 %collective-permute-start.4 = (f32[8,128]{1,0:T(8,128)}, f32[8,128]{1,0:T(8,128)S(1)}, u32[]{:S(2)}, u32[]{:S(2)}) collective-permute-start(f32[8,128]{1,0:T(8,128)} %get-tuple-element.28), channel_id=1, source_target_pairs={{0,8},{8,16},{16,24},{24,0},{1,9},{9,17},{17,25},{25,1},{2,10},{10... | collective-permute-start | bytes 12296 | tf_op jit(solution)/shard_map/ppermute | solution.py:244
  63.5 3.6 %collective-permute-start.5 = (f32[8,128]{1,0:T(8,128)S(1)}, f32[8,128]{1,0:T(8,128)S(1)}, u32[]{:S(2)}, u32[]{:S(2)}) collective-permute-start(f32[8,128]{1,0:T(8,128)S(1)} %copy-done.16), channel_id=1, source_target_pairs={{8,0},{16,8},{24,16},{0,24},{9,1},{17,9},{25,17},{1,25},{10,2},{18... | collective-permute-start | bytes 12296 | tf_op jit(solution)/shard_map/ppermute | solution.py:245
  67.0 0.6 copy-start.8
  67.1 0.6 copy-start.10
  67.1 0.7 copy-start.1
  67.1 0.7 copy-start.3
  71.4 7.3 %copy-start.14 = (f32[8,128]{1,0:T(8,128)S(1)}, f32[8,128]{1,0:T(8,128)}, u32[]{:S(2)}) copy-start(f32[8,128]{1,0:T(8,128)} %get-tuple-element.35) | copy-start | bytes 12292
  71.4 11.0 %collective-permute-start.6 = (f32[256,128]{1,0:T(8,128)}, f32[256,128]{1,0:T(8,128)S(1)}, u32[]{:S(2)}, u32[]{:S(2)}) collective-permute-start(f32[256,128]{1,0:T(8,128)} %get-tuple-element.32), channel_id=1, source_target_pairs={{0,1},{1,2},{2,3},{3,4},{4,5},{5,6},{6,7},{8,9},{9,10},{10,11},{11... | collective-permute-start | bytes 393224 | tf_op jit(solution)/shard_map/ppermute | solution.py:242
  76.3 6.1 %collective-permute-start.7 = (f32[256,128]{1,0:T(8,128)}, f32[256,128]{1,0:T(8,128)S(1)}, u32[]{:S(2)}, u32[]{:S(2)}) collective-permute-start(f32[256,128]{1,0:T(8,128)} %get-tuple-element.33), channel_id=1, source_target_pairs={{1,0},{2,1},{3,2},{4,3},{5,4},{6,5},{7,6},{9,8},{10,9},{11,10},{12... | collective-permute-start | bytes 393224 | tf_op jit(solution)/shard_map/ppermute | solution.py:243
  77.6 4.8 %collective-permute-start.8 = (f32[8,128]{1,0:T(8,128)}, f32[8,128]{1,0:T(8,128)S(1)}, u32[]{:S(2)}, u32[]{:S(2)}) collective-permute-start(f32[8,128]{1,0:T(8,128)} %get-tuple-element.34), channel_id=1, source_target_pairs={{0,8},{8,16},{16,24},{24,0},{1,9},{9,17},{17,25},{25,1},{2,10},{10... | collective-permute-start | bytes 12296 | tf_op jit(solution)/shard_map/ppermute | solution.py:244
  78.7 3.7 %collective-permute-start.9 = (f32[8,128]{1,0:T(8,128)S(1)}, f32[8,128]{1,0:T(8,128)S(1)}, u32[]{:S(2)}, u32[]{:S(2)}) collective-permute-start(f32[8,128]{1,0:T(8,128)S(1)} %copy-done.14), channel_id=1, source_target_pairs={{8,0},{16,8},{24,16},{0,24},{9,1},{17,9},{25,17},{1,25},{10,2},{18... | collective-permute-start | bytes 12296 | tf_op jit(solution)/shard_map/ppermute | solution.py:245
  82.4 0.6 copy-start.9
  82.4 0.6 copy-start.12
  82.4 0.7 copy-start.2
  82.4 0.7 copy-start.5
  86.7 7.8 %copy-start.15 = (f32[8,128]{1,0:T(8,128)S(1)}, f32[8,128]{1,0:T(8,128)}, u32[]{:S(2)}) copy-start(f32[8,128]{1,0:T(8,128)} %get-tuple-element.41) | copy-start | bytes 12292
  86.7 11.4 %collective-permute-start.10 = (f32[256,128]{1,0:T(8,128)}, f32[256,128]{1,0:T(8,128)S(1)}, u32[]{:S(2)}, u32[]{:S(2)}) collective-permute-start(f32[256,128]{1,0:T(8,128)} %get-tuple-element.38), channel_id=1, source_target_pairs={{0,1},{1,2},{2,3},{3,4},{4,5},{5,6},{6,7},{8,9},{9,10},{10,11},{11... | collective-permute-start | bytes 393224 | tf_op jit(solution)/shard_map/ppermute | solution.py:242
  91.0 7.1 %collective-permute-start.11 = (f32[256,128]{1,0:T(8,128)}, f32[256,128]{1,0:T(8,128)S(1)}, u32[]{:S(2)}, u32[]{:S(2)}) collective-permute-start(f32[256,128]{1,0:T(8,128)} %get-tuple-element.39), channel_id=1, source_target_pairs={{1,0},{2,1},{3,2},{4,3},{5,4},{6,5},{7,6},{9,8},{10,9},{11,10},{12... | collective-permute-start | bytes 393224 | tf_op jit(solution)/shard_map/ppermute | solution.py:243
  92.3 4.8 %collective-permute-start.12 = (f32[8,128]{1,0:T(8,128)}, f32[8,128]{1,0:T(8,128)S(1)}, u32[]{:S(2)}, u32[]{:S(2)}) collective-permute-start(f32[8,128]{1,0:T(8,128)} %get-tuple-element.40), channel_id=1, source_target_pairs={{0,8},{8,16},{16,24},{24,0},{1,9},{9,17},{17,25},{25,1},{2,10},{10... | collective-permute-start | bytes 12296 | tf_op jit(solution)/shard_map/ppermute | solution.py:244
  94.5 3.6 %collective-permute-start.13 = (f32[8,128]{1,0:T(8,128)S(1)}, f32[8,128]{1,0:T(8,128)S(1)}, u32[]{:S(2)}, u32[]{:S(2)}) collective-permute-start(f32[8,128]{1,0:T(8,128)S(1)} %copy-done.15), channel_id=1, source_target_pairs={{8,0},{16,8},{24,16},{0,24},{9,1},{17,9},{25,17},{1,25},{10,2},{18... | collective-permute-start | bytes 12296 | tf_op jit(solution)/shard_map/ppermute | solution.py:245
  97.1 1.1 copy-start.11
  98.1 0.6 copy-start.13
  98.1 0.7 copy-start.4
  98.1 0.7 copy-start.6
where the time goes:
time: 156 us; the launch traced here: 155 us
  blocking collectives  64.1 us (41%)
  starting transfers between devices  33.3 us (21%)
  Pallas kernels  26.2 us (17%)
  waiting for transfers between devices  19.6 us (13%)
  local copies, waits for them, and re-layouts  11.3 us (7%)
    all_gather x1, blocking collectives, body(): every = lax.all_gather(sums, ('lon', 'lat'))  46.4 us
    all_to_all x1, blocking collectives, body(): turned = lax.all_to_all(turned, 'lon', 1, 0, tiled=True)  17.7 us
    all_to_all x1, waiting for transfers between devices, body(): piece = lax.all_to_all(mixed, 'lon', 0, 1, tiled=True)  12.1 us
    ppermute x3, starting transfers between devices, halo(): lax.ppermute(last, 'lat', up)  10.9 us
    pallas_call x1, Pallas kernels, body(): call(functools.partial(final_kernel, rows), [whole] * 3, [VM] * 8)  5.67 us
    ppermute x3, waiting for transfers between devices, halo(): lax.ppermute(high, 'lon', east)  5.37 us
    all_to_all x1, starting transfers between devices, body(): piece = lax.all_to_all(mixed, 'lon', 0, 1, tiled=True)  5.19 us
    ppermute x3, starting transfers between devices, halo(): lax.ppermute(high, 'lon', east)  4.56 us
  transfers between devices with their start and end apart: 15, of which 7 were waited for; matrix products, arithmetic and copies ran while one was open for 1% of the time, Pallas kernels for 0%

commit v1 on v0

--- a/solution.py
+++ b/solution.py
@@ -26,16 +26,106 @@
     return jax.ShapeDtypeStruct(dims, F32)
 
 
-def mix_kernel(rows, fr_lat, fr_lev, t_ref, prev_ref, next_ref, out_ref):
+def greet(peers):
+    barrier = pltpu.get_barrier_semaphore()
+    for peer in peers:
+        pl.semaphore_signal(barrier, inc=1, device_id=peer, device_id_type=pl.DeviceIdType.MESH)
+    pl.semaphore_wait(barrier, len(peers))
+
+
+def send(src, dst, send_sem, recv_sem, peer):
+    copy = pltpu.make_async_remote_copy(
+        src_ref=src,
+        dst_ref=dst,
+        send_sem=send_sem,
+        recv_sem=recv_sem,
+        device_id=peer,
+        device_id_type=pl.DeviceIdType.MESH,
+    )
+    copy.start()
+    return copy
+
+
+def around(axis, count, k):
+    return {axis: lax.rem(lax.axis_index(axis) + (k + count), count)}
+
+
+def exchange_kernel(moves, counts, *refs):
+    n = len(moves)
+    ins, outs, send_sem, recv_sem = refs[:n], refs[n : 2 * n], refs[-2], refs[-1]
+    peers = [around(axis, counts[axis], k) for axis, k in moves]
+    greet(peers)
+    copies = [send(ins[i], outs[i], send_sem.at[i], recv_sem.at[i], peers[i]) for i in range(n)]
+    for copy in copies:
+        copy.wait()
+
+
+def turn_kernel(count, some, width, back, x_ref, out_ref, send_sem, recv_sem, own_sem):
+    me = lax.axis_index("lon")
+
+    def rows_at(ref, d):
+        return ref.at[pl.ds(d * some, some)]
+
+    def cells_at(ref, d):
+        return ref.at[:, pl.ds(pl.multiple_of(d * width, width), width), :]
+
+    take, give = (cells_at, rows_at) if back else (rows_at, cells_at)
+    own = pltpu.make_async_copy(take(x_ref, me), give(out_ref, me), own_sem)
+    own.start()
+    peers = [around("lon", count, k) for k in range(1, count)]
+    greet(peers)
+    copies = [
+        send(take(x_ref, p["lon"]), give(out_ref, me), send_sem.at[i], recv_sem.at[i], p)
+        for i, p in enumerate(peers)
+    ]
+    for copy in copies:
+        copy.wait()
+    own.wait()
+
+
+def collect_kernel(lons, lats, x_ref, out_ref, send_sem, recv_sem, own_sem):
+    a, b = lax.axis_index("lon"), lax.axis_index("lat")
+    own = pltpu.make_async_copy(x_ref, out_ref.at[a, b], own_sem)
+    own.start()
+    first = [around("lat", lats, k) for k in range(1, lats)]
+    second = [around("lon", lons, k) for k in range(1, lons)]
+    greet(first + second)
+    copies = [
+        send(x_ref, out_ref.at[a, b], send_sem.at[i], recv_sem.at[i], p) for i, p in enumerate(first)
+    ]
+    for copy in copies:
+        copy.wait()
+    own.wait()
+    copies = [
+        send(out_ref.at[a], out_ref.at[a], send_sem.at[lats - 1 + i], recv_sem.at[lats - 1 + i], p)
+        for i, p in enumerate(second)
+    ]
+    for copy in copies:
+        copy.wait()
+
+
+def talk(kernel, outs, n_in, sems, number, own):
+    dma = pltpu.SemaphoreType.DMA
+    return pl.pallas_call(
+        kernel,
+        out_shape=outs,
+        in_specs=[VM] * n_in,
+        out_specs=jax.tree.map(lambda _: VM, outs),
+        scratch_shapes=[dma((sems,)), dma((sems,))] + [dma] * own,
+        compiler_params=pltpu.CompilerParams(collective_id=number, has_side_effects=True),
+    )
+
+
+def mix_kernel(rows, keep, fr_lat, fr_lev, t_ref, prev_ref, next_ref, out_ref):
     width, levels = prev_ref.shape
     lane = lax.broadcasted_iota(jnp.int32, (1, levels), 1)
-    row = [prev_ref[...]]
+    row = [keep[0] * prev_ref[...]]
     row += [t_ref[pl.ds(j, width, stride=rows), :] for j in range(2)]
     for j in range(rows):
         if j + 2 < rows:
             row.append(t_ref[pl.ds(j + 2, width, stride=rows), :])
         else:
-            row.append(next_ref[j + 2 - rows])
+            row.append(keep[1] * next_ref[j + 2 - rows])
         a = cubic_weights(fr_lat[j])
         b = cubic_weights(fr_lev[j])
         lat = a[0] * row[j] + a[1] * row[j + 1] + a[2] * row[j + 2] + a[3] * row[j + 3]
@@ -93,7 +183,7 @@
         put(outs, j, rows, solve_lines(inv_ref[j], r_ref[j]))
 
 
-def apply_row(j, rows, metric, vc_ref, w_ref, prev, nxt, west, east, pad):
+def apply_row(j, rows, keep, metric, vc_ref, w_ref, prev, nxt, west, east, pad):
     width, levels = prev.shape
     lane = lax.broadcasted_iota(jnp.int32, (1, levels), 1)
     vc = vc_ref[...]
@@ -103,8 +193,8 @@
     pad[7:8, :] = west[j : j + 1, :]
     pad[8 : 8 + width, :] = w
     pad[8 + width : 9 + width, :] = east[j : j + 1, :]
-    south = prev[...] if j == 0 else w_ref[j - 1]
-    north = nxt[...] if j == rows - 1 else w_ref[j + 1]
+    south = keep[0] * prev[...] if j == 0 else w_ref[j - 1]
+    north = keep[1] * nxt[...] if j == rows - 1 else w_ref[j + 1]
     m = metric[j]
     result = (2.0 * m + 2.1 + 2.0 * vc) * w
     result = result - m * (pad[9 : 9 + width, :] + pad[7 : 7 + width, :])
@@ -113,19 +203,19 @@
     return result - down * pltpu.roll(w, 1, 1)
 
 
-def apply_kernel(rows, metric, vc, inv_ref, w_ref, prev, nxt, west, east, v_ref, *rest):
+def apply_kernel(rows, keep, metric, vc, inv_ref, w_ref, prev, nxt, west, east, v_ref, *rest):
     outs, pad = rest[:-1], rest[-1]
     for j in range(rows):
-        v = apply_row(j, rows, metric, vc, w_ref, prev, nxt, west, east, pad.at[j % 2])
+        v = apply_row(j, rows, keep, metric, vc, w_ref, prev, nxt, west, east, pad.at[j % 2])
         v_ref[j] = v
         put(outs, j, rows, solve_lines(inv_ref[j], v))
 
 
-def last_kernel(rows, metric, vc, r_ref, v0_ref, v1_ref, w_ref, prev, nxt, west, east, v_ref, sums, pad):
+def last_kernel(rows, keep, metric, vc, r_ref, v0_ref, v1_ref, w_ref, prev, nxt, west, east, v_ref, sums, pad):
     levels = prev.shape[1]
     acc = [jnp.zeros((1, levels), F32) for _ in range(9)]
     for j in range(rows):
-        v2 = apply_row(j, rows, metric, vc, w_ref, prev, nxt, west, east, pad.at[j % 2])
+        v2 = apply_row(j, rows, keep, metric, vc, w_ref, prev, nxt, west, east, pad.at[j % 2])
         v_ref[j] = v2
         r, v0, v1 = r_ref[j], v0_ref[j], v1_ref[j]
         pairs = [(r, v0), (r, v1), (r, v2), (v0, v0), (v0, v1), (v0, v2), (v1, v1), (v1, v2), (v2, v2)]
@@ -199,22 +289,29 @@
     width, rows, levels = tracer.shape
     lons, lats = lax.axis_size("lon"), lax.axis_size("lat")
     cells = width * lons
-    up = [(i, i + 1) for i in range(lats - 1)]
-    down = [(i + 1, i) for i in range(lats - 1)]
-    east = [(i, (i + 1) % lons) for i in range(lons)]
-    west = [((i + 1) % lons, i) for i in range(lons)]
+    counts = {"lon": lons, "lat": lats}
+    lat = lax.axis_index("lat")
+    keep = jnp.stack([lat > 0, lat < lats - 1]).astype(F32)
+
+    def exchange(number, arrays, moves):
+        kernel = functools.partial(exchange_kernel, moves, counts)
+        outs = [shape(*x.shape) for x in arrays]
+        return talk(kernel, outs, len(arrays), len(arrays), number, 0)(*arrays)
+
     flat = tracer.reshape(width * rows, levels)
-    prev = lax.ppermute(tracer[:, rows - 1, :], "lat", up)
-    nxt = lax.ppermute(jnp.stack([tracer[:, 0, :], tracer[:, 1, :]]), "lat", down)
+    ends = (tracer[:, rows - 1, :], jnp.stack([tracer[:, 0, :], tracer[:, 1, :]]))
+    prev, nxt = exchange(1, ends, (("lat", 1), ("lat", -1)))
     cube = shape(rows, width, levels)
-    mixed = call(functools.partial(mix_kernel, rows), cube, [SM, SM, VM, VM, VM])(
-        frac_lat, frac_lev, flat, prev, nxt
+    mixed = call(functools.partial(mix_kernel, rows), cube, [SM, SM, SM, VM, VM, VM])(
+        keep, frac_lat, frac_lev, flat, prev, nxt
     )
     chunk = min(128, width)
     lon = lax.axis_index("lon")
     if rows % lons == 0:
         some = rows // lons
-        piece = lax.all_to_all(mixed, "lon", 0, 1, tiled=True)
+        turn = functools.partial(turn_kernel, lons, some, width)
+        turned_shape = shape(some, cells, levels)
+        piece = talk(functools.partial(turn, False), turned_shape, 1, lons - 1, 2, 1)(mixed)
         mine = lambda x: lax.dynamic_slice_in_dim(x, lon * some, some)
         args = (mine(offsets), mine(frac_lon), jnp.zeros((1,), jnp.int32))
         out = cells
@@ -230,29 +327,29 @@
         [pltpu.VMEM((some, cells + chunk + 8, levels), F32)],
     )(*args, piece)
     if rows % lons == 0:
-        turned = lax.all_to_all(turned, "lon", 1, 0, tiled=True)
+        turned = talk(functools.partial(turn, True), cube, 1, lons - 1, 3, 1)(turned)
     r0 = turned
     vc = vertical_coef.reshape(1, levels)
     edge, end = shape(width, levels), shape(rows, levels)
     fields = [cube, edge, edge, end, end]
     pad = [pltpu.VMEM((2, width + 16, levels), F32)]
 
-    def halo(first, last, low, high):
-        return (
-            lax.ppermute(last, "lat", up),
-            lax.ppermute(first, "lat", down),
-            lax.ppermute(high, "lon", east),
-            lax.ppermute(low, "lon", west),
-        )
+    moves = (("lat", -1), ("lat", 1), ("lon", -1), ("lon", 1))
+
+    def halo(number, first, last, low, high):
+        nxt, prev, east, west = exchange(number, (first, last, low, high), moves)
+        return prev, nxt, west, east
 
     w0, *edges = call(functools.partial(line_kernel, rows), fields, [VM, VM])(inverses, r0)
-    step = call(functools.partial(apply_kernel, rows), [cube] + fields, [SM] + [VM] * 7, pad)
-    v0, w1, *edges = step(metric, vc, inverses, w0, *halo(*edges))
-    v1, w2, *edges = step(metric, vc, inverses, w1, *halo(*edges))
+    step = call(functools.partial(apply_kernel, rows), [cube] + fields, [SM, SM] + [VM] * 7, pad)
+    v0, w1, *edges = step(keep, metric, vc, inverses, w0, *halo(4, *edges))
+    v1, w2, *edges = step(keep, metric, vc, inverses, w1, *halo(5, *edges))
     v2, sums = call(
-        functools.partial(last_kernel, rows), [cube, shape(16, levels)], [SM] + [VM] * 9, pad
-    )(metric, vc, r0, v0, v1, w2, *halo(*edges))
-    every = lax.all_gather(sums, ("lon", "lat"))
+        functools.partial(last_kernel, rows), [cube, shape(16, levels)], [SM, SM] + [VM] * 9, pad
+    )(keep, metric, vc, r0, v0, v1, w2, *halo(6, *edges))
+    collect = functools.partial(collect_kernel, lons, lats)
+    every = talk(collect, shape(lons, lats, 16, levels), 1, lons + lats - 2, 7, 1)(sums)
+    every = every.reshape(lons * lats, 16, levels)
     whole = shape(width * rows, levels)
     outs = call(functools.partial(final_kernel, rows), [whole] * 3, [VM] * 8)(
         every, r0, v0, v1, v2, w0, w1, w2

time: 156 us -> 115 us (0.74)
  Pallas kernels: 26.2 us -> 107 us
  blocking collectives: 64.1 us -> 0 us
  starting transfers between devices: 33.3 us -> 0 us
  waiting for transfers between devices: 19.6 us -> 0 us
  local copies, waits for them, and re-layouts: 11.3 us -> 4.71 us
    pallas_call x3 -> x10, Pallas kernels: 10.5 us -> 91.8 us  [the longest x4 36.1 us: exchange(): return talk(kernel, outs, len(arrays), len(arrays), number, 0)(*arrays)]
    all_gather x1 -> x0, blocking collectives: 46.4 us -> none  [body(): every = lax.all_gather(sums, ('lon', 'lat'))]
    ppermute x14 -> x0, starting transfers between devices: 28.1 us -> none  [the longest x3 10.9 us: halo(): lax.ppermute(last, 'lat', up)]
    all_to_all x1 -> x0, blocking collectives: 17.7 us -> none  [body(): turned = lax.all_to_all(turned, 'lon', 1, 0, tiled=True)]
    all_to_all x1 -> x0, waiting for transfers between devices: 12.1 us -> none  [body(): piece = lax.all_to_all(mixed, 'lon', 0, 1, tiled=True)]
    ppermute x14 -> x0, waiting for transfers between devices: 7.55 us -> none  [the longest x3 5.37 us: halo(): lax.ppermute(high, 'lon', east)]
    all_to_all x1 -> x0, starting transfers between devices: 5.19 us -> none  [body(): piece = lax.all_to_all(mixed, 'lon', 0, 1, tiled=True)]
    unnamed x38 -> x4, local copies, waits for them, and re-layouts: 3.52 us -> 0.73 us
  transfers between devices with their start and end apart: 15 -> 0, of which waited for: 7 -> 0; matrix products, arithmetic and copies ran while one was open for 1% -> 0% of each run, Pallas kernels for 0% -> 0%
where the time goes in v1:
time: 115 us; the launch traced here: 114 us
  Pallas kernels  107 us (93%)
  local copies, waits for them, and re-layouts  4.71 us (4%)
  other arithmetic  1.33 us (1%)
    pallas_call x4, Pallas kernels, exchange(): return talk(kernel, outs, len(arrays), len(arrays), number, 0)(*arrays)  36.1 us
    pallas_call x1, Pallas kernels, body(): talk(functools.partial(turn, True), cube, 1, lons - 1, 3, 1)(turned)  17 us
    pallas_call x1, Pallas kernels, body(): talk(functools.partial(turn, False), turned_shape, 1, lons - 1, 2, 1)(mixed)  16.7 us
    pallas_call x1, Pallas kernels, body(): talk(collect, shape(lons, lats, 16, levels), 1, lons + lats - 2, 7, 1)(sums)  11.4 us
    pallas_call x1, Pallas kernels, body(): call(functools.partial(final_kernel, rows), [whole] * 3, [VM] * 8)  5.68 us
    pallas_call x1, Pallas kernels, body(): call(functools.partial(last_kernel, rows), [cube, shape(16, levels)], [SM...  4.35 us
    pallas_call x1, Pallas kernels, body(): v0, w1, *edges = step(keep, metric, vc, inverses, w0, *halo(4, *edges))  3.61 us
    pallas_call x1, Pallas kernels, body(): v1, w2, *edges = step(keep, metric, vc, inverses, w1, *halo(5, *edges))  3.6 us

profile of v1, /device:TPU:0, one launch (start us, length us, event | category | flops | bytes accessed | tf_op | source)
XLA Modules:
  0.0 114.2 jit_solution(3473903758976649889)
XLA Ops:
  0.6 0.6 add_convert_fusion.keep
  1.3 0.0 copy-start
  1.3 0.7 copy-done
  1.9 0.0 copy-start.1
  1.9 0.6 dynamic_slice.6.off
  2.5 0.1 copy-done.1
  2.6 0.6 dynamic_slice.7.fr
  3.1 2.8 %fusion = (f32[256,1,128]{2,1,0:T(1,128)S(1)}, f32[256,1,128]{2,1,0:T(1,128)}, f32[256,1,128]{2,1,0:T(1,128)S(1)}) fusion(f32[256,8,128]{2,1,0:T(8,128)} %param.8), kind=kLoop, calls=%fused_computation.2 | loop fusion | bytes 786432 | tf_op jit(solution)/shard_map/slice | solution.py:302
  6.0 0.7 pad_maximum_fusion.refs_1_
  6.7 10.9 %shard_map.103 = (f32[256,128]{1,0:T(8,128)}, f32[2,256,128]{2,1,0:T(8,128)}) custom-call(f32[256,128]{1,0:T(8,128)} %bitcast.19, f32[2,256,128]{2,1,0:T(8,128)} %pad_maximum_fusion.refs_1_), custom_call_target="tpu_custom_call" | custom-call | tf_op jit(solution)/shard_map/pallas_call | solution.py:299
  17.6 3.3 %shard_map.104.x_ref = f32[8,256,128]{2,1,0:T(8,128)} custom-call(f32[2]{0:T(128)} %add_convert_fusion.keep, f32[8]{0:T(128)} %fr_lat.1, f32[8]{0:T(128)} %fr_lev.1, f32[2048,128]{1,0:T(8,128)} %bitcast.17, f32[256,128]{1,0:T(8,128)} %get-tuple-element.39.prev_ref, f32[2,256,128]{2,1,0:T(8,128)} %get-tuple-element.40.next_ref), custom_call_target="tpu_custom_call" | custom-call | tf_op jit(solution)/shard_map/pallas_call | solution.py:305
  20.9 16.7 %shard_map.105.in_ref = f32[2,1024,128]{2,1,0:T(8,128)} custom-call(f32[8,256,128]{2,1,0:T(8,128)} %shard_map.104.x_ref), custom_call_target="tpu_custom_call" | custom-call | tf_op jit(solution)/shard_map/pallas_call | solution.py:314
  37.6 2.7 %shard_map.106.x_ref = f32[2,1024,128]{2,1,0:T(8,128)} custom-call(s32[2]{0:T(128)} %dynamic_slice.6.off, f32[2]{0:T(128)} %dynamic_slice.7.fr, s32[1]{0:T(128)} %constant.17.clone.1.base, f32[2,1024,128]{2,1,0:T(8,128)} %shard_map.105.in_ref), custom_call_target="tpu_custom_call" | custom-call | tf_op jit(solution)/shard_map/pallas_call | solution.py:323
  40.3 17.0 %shard_map.107.r_ref = f32[8,256,128]{2,1,0:T(8,128)} custom-call(f32[2,1024,128]{2,1,0:T(8,128)} %shard_map.106.x_ref), custom_call_target="tpu_custom_call" | custom-call | tf_op jit(solution)/shard_map/pallas_call | solution.py:330
  57.4 3.0 %shard_map.108 = (f32[8,256,128]{2,1,0:T(8,128)}, f32[256,128]{1,0:T(8,128)}, f32[256,128]{1,0:T(8,128)}, f32[8,128]{1,0:T(8,128)}, f32[8,128]{1,0:T(8,128)}) custom-call(f32[8,128,128]{2,1,0:T(8,128)} %inv_ref.5, f32[8,256,128]{2,1,0:T(8,128)} %shard_map.107.r_ref), custom_call_target="tpu_custom_call" | custom-call | tf_op jit(solution)/shard_map/pallas_call | solution.py:343
  60.3 8.7 %shard_map.109 = (f32[256,128]{1,0:T(8,128)}, f32[256,128]{1,0:T(8,128)}, f32[8,128]{1,0:T(8,128)}, f32[8,128]{1,0:T(8,128)}) custom-call(f32[256,128]{1,0:T(8,128)} %get-tuple-element.42.refs_0_, f32[256,128]{1,0:T(8,128)} %get-tuple-element.43.refs_1_, f32[8,128]{1,0:T(8,128)} %get-tuple-element.44.refs_2_, f32[8,128]{1,0:T(8,128)} %get-tuple-element.45.refs_3_), custom_call_target="tpu_custom_call" | custom-call | tf_op jit(solution)/shard_map/pallas_call | solution.py:299
  69.0 3.6 %shard_map.110 = (f32[8,256,128]{2,1,0:T(8,128)}, f32[8,256,128]{2,1,0:T(8,128)}, f32[256,128]{1,0:T(8,128)}, f32[256,128]{1,0:T(8,128)}, f32[8,128]{1,0:T(8,128)}, /*index=5*/f32[8,128]{1,0:T(8,128)}) custom-call(f32[2]{0:T(128)} %add_convert_fusion.keep, f32[8]{0:T(128)} %metric.5, f32[1,128]{1,0:T(1,128)} %bitcast.22, f32[8,128,128]{2,1,0:T(8,128)} %inv_ref.5, ...), custom_call_target="tpu_custom_call" | custom-call | tf_op jit(solution)/shard_map/pallas_call | solution.py:345
  72.6 8.6 %shard_map.111 = (f32[256,128]{1,0:T(8,128)}, f32[256,128]{1,0:T(8,128)}, f32[8,128]{1,0:T(8,128)}, f32[8,128]{1,0:T(8,128)}) custom-call(f32[256,128]{1,0:T(8,128)} %get-tuple-element.52.refs_0_, f32[256,128]{1,0:T(8,128)} %get-tuple-element.53.refs_1_, f32[8,128]{1,0:T(8,128)} %get-tuple-element.54.refs_2_, f32[8,128]{1,0:T(8,128)} %get-tuple-element.55.refs_3_), custom_call_target="tpu_custom_call" | custom-call | tf_op jit(solution)/shard_map/pallas_call | solution.py:299
  81.2 3.6 %shard_map.112 = (f32[8,256,128]{2,1,0:T(8,128)}, f32[8,256,128]{2,1,0:T(8,128)}, f32[256,128]{1,0:T(8,128)}, f32[256,128]{1,0:T(8,128)}, f32[8,128]{1,0:T(8,128)}, /*index=5*/f32[8,128]{1,0:T(8,128)}) custom-call(f32[2]{0:T(128)} %add_convert_fusion.keep, f32[8]{0:T(128)} %metric.5, f32[1,128]{1,0:T(1,128)} %bitcast.23, f32[8,128,128]{2,1,0:T(8,128)} %inv_ref.5, ...), custom_call_target="tpu_custom_call" | custom-call | tf_op jit(solution)/shard_map/pallas_call | solution.py:346
  84.8 7.9 %shard_map.113 = (f32[256,128]{1,0:T(8,128)}, f32[256,128]{1,0:T(8,128)}, f32[8,128]{1,0:T(8,128)}, f32[8,128]{1,0:T(8,128)}) custom-call(f32[256,128]{1,0:T(8,128)} %get-tuple-element.62.refs_0_, f32[256,128]{1,0:T(8,128)} %get-tuple-element.63.refs_1_, f32[8,128]{1,0:T(8,128)} %get-tuple-element.64.refs_2_, f32[8,128]{1,0:T(8,128)} %get-tuple-element.65.refs_3_), custom_call_target="tpu_custom_call" | custom-call | tf_op jit(solution)/shard_map/pallas_call | solution.py:299
  92.8 4.4 %shard_map.114 = (f32[8,256,128]{2,1,0:T(8,128)}, f32[16,128]{1,0:T(8,128)}) custom-call(f32[2]{0:T(128)} %add_convert_fusion.keep, f32[8]{0:T(128)} %metric.5, f32[1,128]{1,0:T(1,128)} %bitcast.24, f32[8,256,128]{2,1,0:T(8,128)} %shard_map.107.r_ref, f32[8,256,128]{2,1,0:T(8,128)} %get-tuple-element.50.v0_ref.v0, ...), custom_call_target="tpu_custom_call" | custom-call | tf_op jit(solution)/shard_map/pallas_call | solution.py:347
  97.1 11.4 %shard_map.115 = f32[4,8,16,128]{3,2,1,0:T(8,128)} custom-call(f32[16,128]{1,0:T(8,128)} %get-tuple-element.70.x_ref), custom_call_target="tpu_custom_call" | custom-call | tf_op jit(solution)/shard_map/pallas_call | solution.py:351
  108.5 5.7 %shard_map.116 = (f32[2048,128]{1,0:T(8,128)}, f32[2048,128]{1,0:T(8,128)}, f32[2048,128]{1,0:T(8,128)}) custom-call(f32[32,16,128]{2,1,0:T(8,128)} %bitcast.18, f32[8,256,128]{2,1,0:T(8,128)} %shard_map.107.r_ref, f32[8,256,128]{2,1,0:T(8,128)} %get-tuple-element.50.v0_ref.v0, f32[8,256,128]{2,1,0:T(8,128)} %get-tuple-element.60.v1_ref.v1, ...), custom_call_target="tpu_custom_call" | custom-call | tf_op jit(solution)/shard_map/pallas_call | solution.py:354
Async XLA Ops:
  1.3 0.7 copy-start
  1.9 0.7 copy-start.1
